TPU v7x, 32 devices: a whole 2x2x4 slice. The times are simulated.
32 devices in a mesh: shot: 2 (over core), probe: 16 (over z, y, x).
Axes of the slice: x: 2, y: 2, z: 4, core: 2. Of those that a mesh axis runs over, the one named last changes fastest.
Arguments:
- probes: float32 [32, 256, 512], P('probe'), may hold values from -6 to 6
- coarse_sample: float32 [32, 256, 512], P('probe', 'shot'), may hold values from -6 to 6
- coefficient: float32 [256, 512], replicated, may hold values from 0.05 to 0.45
- receiver: float32 [256, 512], replicated, may hold values from 0.05 to 0.5
- checkpoints: float32 [4, 2, 256, 512], P('shot', None, 'probe'), may hold values from -6 to 6
- encodings: int32 [4, 256], P('shot'), may hold values from -1 to 1, as said below
- wavelet: float32 [3, 256], replicated, may hold values from -6 to 6
- bounds: int32 [33], replicated, may hold values from 0 to 256, as said below
Outputs:
- samples: float32 [32, 256, 512], P('probe', 'shot')
Inputs may be any that keep to these rules, and one draw needn't show every extreme that they name: `encodings`: every entry is -1 or 1. bounds[0] = 0 and bounds[32] = 256; the entries rise strictly; blocks 2 i and 2 i + 1 together hold exactly 16 rows.
All inputs are finite; a program needn't handle non-finite values.
Results may differ from a plain program's by a relative error of at most 0.000094.
Values sent between devices are 32-bit elements; how exact they have to be, the bound alone decides.
A program may use at most 128 MiB of HBM per device.

v0:
```python
import jax
import jax.numpy as jnp
from jax import lax
from jax.sharding import PartitionSpec as P

NZ = 512
NSHOT = 256
NT = 4


def laplace(values):
    pad_width = [(0, 0)] * (values.ndim - 2) + [(1, 1), (1, 1)]
    padded = jnp.pad(values, pad_width)
    return (
        padded[..., 2:, 1:-1]
        + padded[..., :-2, 1:-1]
        + padded[..., 1:-1, 2:]
        + padded[..., 1:-1, :-2]
        - 4.0 * values
    )


def shot_sources(encodings, wavelet):
    columns = jnp.arange(NZ)
    spacing = NZ // NSHOT
    position = jnp.arange(NSHOT) * NZ // NSHOT + spacing // 2
    onehot = (position[:, None] == columns[None, :]).astype(jnp.float32)
    amplitude = encodings.astype(jnp.float32)[:, None, :] * wavelet[None, :, :]
    return jnp.einsum("stk,kz->stz", amplitude, onehot, precision=lax.Precision.HIGHEST)


def block_parity(row_index, bounds):
    inner = bounds[1:-1]
    return jnp.sum((row_index[:, None] >= inner[None, :]).astype(jnp.int32), axis=1) % 2


def hessian_term(vectors, levels, coefficient, weight_square):
    before = jnp.zeros_like(vectors)
    current = jnp.zeros_like(vectors)
    deltas = []
    for moment in range(NT):
        following = (
            2.0 * current - before + coefficient * laplace(current) + vectors * levels[moment]
        )
        before, current = (current, following)
        deltas.append(following)
    upcoming = jnp.zeros_like(vectors)
    beyond = jnp.zeros_like(vectors)
    gradient = jnp.zeros_like(vectors)
    for moment in range(NT, 0, -1):
        adjoint = (
            weight_square * deltas[moment - 1]
            + 2.0 * upcoming
            + laplace(coefficient * upcoming)
            - beyond
        )
        gradient = gradient + levels[moment - 1] * adjoint
        beyond, upcoming = (upcoming, adjoint)
    return gradient


def on_device(
    probes, coarse_sample, coefficient, receiver, checkpoints, encodings, wavelet, bounds
):
    num_rows = probes.shape[1]
    source_at = num_rows // 2
    sources = shot_sources(encodings, wavelet)
    colour = jnp.arange(probes.shape[0]) % 2
    parity_all = block_parity(jnp.arange(num_rows), bounds)
    support = (parity_all[None, :] == colour[:, None]).astype(jnp.float32)
    vectors = probes * support[:, :, None]
    weight_square = receiver * receiver
    accumulated = jnp.zeros_like(probes)
    for member in range(checkpoints.shape[0]):
        stored = lax.all_gather(checkpoints[member], "probe", axis=1, tiled=True)
        at_source = (jnp.arange(num_rows) == source_at).astype(jnp.float32)[:, None]
        before = stored[0]
        current = stored[1]
        history = [current]
        for moment in range(NT - 1):
            following = (
                2.0 * current
                - before
                + coefficient * laplace(current)
                + at_source * sources[member, moment][None, :]
            )
            before, current = (current, following)
            history.append(current)
        levels = jnp.stack(history)
        accumulated = accumulated + hessian_term(vectors, levels, coefficient, weight_square)
    out_rows = coarse_sample.shape[1]
    summed = lax.psum(accumulated, "shot")
    share = lax.dynamic_slice_in_dim(summed, lax.axis_index("shot") * out_rows, out_rows, 1)
    row_out = lax.axis_index("shot") * out_rows + jnp.arange(out_rows)
    keep = (block_parity(row_out, bounds)[None, :] != colour[:, None]).astype(jnp.float32)
    return keep[:, :, None] * (share - coarse_sample)


def solution(mesh):
    return jax.shard_map(
        on_device,
        mesh=mesh,
        in_specs=(
            P("probe", None, None),
            P("probe", "shot", None),
            P(),
            P(),
            P("shot", None, "probe", None),
            P("shot", None),
            P(),
            P(),
        ),
        out_specs=P("probe", "shot", None),
        check_vma=False,
    )
```

profile of v0, /device:TPU:0, one launch (start us, length us, event | category | flops | bytes accessed | tf_op | source)
XLA Modules:
  0.0 186.1 jit_solution(16880601217154744731)
XLA Ops:
  6.5 1.5 fusion.153
  8.1 0.7 all-gather.5.cloned.1.call-update
  8.9 0.7 convert_element_type.69
  9.6 0.7 slice.296
  10.3 1.4 mul.554
  12.3 55.9 %all-gather.7.cloned.1.call-done = f32[1,2,256,512]{3,2,1,0:T(8,128)} async-done(((f32[1,2,16,512]{3,2,1,0:T(8,128)}), f32[1,2,256,512]{3,2,1,0:T(8,128)}) %all-gather.7.cloned.1.call-update) | async-done | bytes 1048592 | tf_op jit(solution)/shard_map/all_gather | solution.py:75
  68.2 1.2 slice_bitcast_fusion.1
  69.4 55.8 %all-gather.5.cloned.1.call-done = f32[1,2,256,512]{3,2,1,0:T(8,128)} async-done(((f32[1,2,16,512]{3,2,1,0:T(8,128)}), f32[1,2,256,512]{3,2,1,0:T(8,128)}) %all-gather.5.cloned.1.call-update) | async-done | bytes 1048592 | tf_op jit(solution)/shard_map/all_gather | solution.py:75
  125.2 1.1 slice_bitcast_fusion.3
  126.3 1.9 %fusion.116 = (f32[256,512]{1,0:T(8,128)S(1)}, f32[256,512]{1,0:T(8,128)S(1)}) fusion(f32[256,512]{1,0:T(8,128)S(1)} %copy-done, f32[256,512]{1,0:T(8,128)S(1)} %slice_bitcast_fusion.1, f32[1,2,256,512]{3,2,1,0:T(8,128)S(1)} %copy-done.20, f32[512]{0:T(512)S(1)} %bitcast.33, f32[256]{0:T(256)S(1)} %compare_convert_fusion.1, f32[512]{0:T(512)S(1)} %bitcast.34, ...), kind=kLoop, calls=%fused_computation.198 | loop fusion | flops 2883584 | bytes 3675136 | tf_op jit(solution)/shard_map/add | solution.py:82
  128.2 0.8 fusion.123
  129.2 1.1 fusion.130
  130.3 0.4 copy-done.1
  131.1 0.8 fusion.49
  131.8 1.5 fusion.56
  133.3 0.9 fusion.13
  134.3 0.3 fusion.109
  134.6 3.2 %broadcast_multiply_fusion.2 = (f32[2,256,512]{2,1,0:T(8,128)S(1)}, f32[2,256,512]{2,1,0:T(8,128)S(1)}, f32[2,256,512]{2,1,0:T(8,128)}, f32[2,256,512]{2,1,0:T(8,128)S(1)}) fusion(f32[256,512]{1,0:T(8,128)S(1)} %copy-done, f32[256,512]{1,0:T(8,128)S(1)} %fusion.109, f32[256,512]{1,0:T(8,128)S(1)} %get-tuple-element.25, f32[2,256,512]{2,1,0:T(8,128)S(1)} %copy-done.1, ...), kind=kLoop, calls=%fused_computation.226 | loop fusion | flops 7602176 | bytes 12060672 | tf_op jit(solution)/shard_map/mul | solution.py:54
  137.9 2.2 %broadcast_multiply_fusion.1 = (f32[2,256,512]{2,1,0:T(8,128)}, f32[2,256,512]{2,1,0:T(8,128)}) fusion(f32[256,512]{1,0:T(8,128)S(1)} %copy-done, f32[2,256,512]{2,1,0:T(8,128)S(1)} %get-tuple-element.9, f32[2,256,512]{2,1,0:T(8,128)S(1)} %get-tuple-element.10, f32[2,256,512]{2,1,0:T(8,128)S(1)} %get-tuple-element.19, f32[256,512]{1,0:T(8,128)S(1)} %mul.554), kind=kLoop, calls=%fused_computation.225 | loop fusion | flops 2621440 | bytes 6291456 | tf_op jit(solution)/shard_map/mul | solution.py:54
  140.0 9.3 %broadcast_multiply_fusion = (f32[2,256,512]{2,1,0:T(8,128)}, f32[2,256,512]{2,1,0:T(8,128)}, f32[2,256,512]{2,1,0:T(8,128)}, f32[2,256,512]{2,1,0:T(8,128)}) fusion(f32[256,512]{1,0:T(8,128)S(1)} %copy-done, f32[2,256,512]{2,1,0:T(8,128)S(1)} %get-tuple-element.10, f32[2,256,512]{2,1,0:T(8,128)} %get-tuple-element.7, f32[2,256,512]{2,1,0:T(8,128)} %get-tuple-element.8, ...), kind=kLoop, calls=%fused_computation.224 | loop fusion | flops 5505024 | bytes 12582912 | tf_op jit(solution)/shard_map/mul | solution.py:54
  149.4 4.6 %broadcast_multiply_fusion.3 = (f32[2,256,512]{2,1,0:T(8,128)S(1)}, f32[2,256,512]{2,1,0:T(8,128)S(1)}) fusion(f32[256,512]{1,0:T(8,128)S(1)} %copy-done, f32[2,256,512]{2,1,0:T(8,128)S(1)} %get-tuple-element.18, f32[2,256,512]{2,1,0:T(8,128)} %get-tuple-element.23, f32[2,256,512]{2,1,0:T(8,128)} %get-tuple-element.24, ...), kind=kLoop, calls=%fused_computation.227 | loop fusion | flops 2883584 | bytes 7340032 | tf_op jit(solution)/shard_map/mul | solution.py:54
  154.2 4.9 %fusion.42 = f32[2,256,512]{2,1,0:T(8,128)} fusion(f32[2,256,512]{2,1,0:T(8,128)S(1)} %copy-done.4, f32[2,256,512]{2,1,0:T(8,128)S(1)} %get-tuple-element.11, f32[2,256,512]{2,1,0:T(8,128)S(1)} %copy-done.6, f32[2,256,512]{2,1,0:T(8,128)S(1)} %copy-done.19, f32[2,256,512]{2,1,0:T(8,128)} %get-tuple-element.6, f32[2,256,512]{2,1,0:T(8,128)S(1)} %get-tuple-element.21, ...), kind=kLoop, calls=%fused_computation.94 | loop fusion | flops 9175040 | bytes 16252928 | tf_op jit(solution)/shard_map/add | solution.py:90
  159.4 18.3 %all-reduce.22.cloned.1.call-done = f32[2,256,512]{2,1,0:T(8,128)} async-done(((f32[2,256,512]{2,1,0:T(8,128)}), f32[2,256,512]{2,1,0:T(8,128)}) %all-reduce.22.cloned.1.call-update) | async-done | bytes 1048592 | tf_op jit(solution)/shard_map/psum | solution.py:92
  177.6 1.9 %subtract_multiply_fusion = f32[2,128,512]{2,1,0:T(8,128)} fusion(f32[2,128,512]{2,1,0:T(8,128)S(1)} %copy-done.22, f32[2,256,512]{2,1,0:T(8,128)} %all-reduce.22.cloned.1.call-done, s32[]{:T(128)S(6)} %select_n.49, f32[2,128]{1,0:T(2,128)S(1)} %compare_convert_fusion.2), kind=kLoop, calls=%fused_computation.223 | loop fusion | flops 262144 | bytes 1573892 | tf_op jit(solution)/shard_map/mul | solution.py:96
  (66 shorter events, 1.4 us)
Async XLA Ops:
  6.5 5.4 %copy-start.23 = (f32[3,256]{1,0:T(4,128)S(1)}, f32[3,256]{1,0:T(4,128)}, u32[]{:S(2)}) copy-start(f32[3,256]{1,0:T(4,128)} %param.14) | copy-start | bytes 9220
  6.5 61.6 %all-gather.7.cloned.1.call-start = ((), (), s32[]{:S(2)}) async-start(), calls=%async_computation.2 | async-start | bytes 1114112 | tf_op jit(solution)/shard_map/all_gather | solution.py:75
  8.1 117.1 %all-gather.5.cloned.1.call-start = ((), (), s32[]{:S(2)}) async-start(), calls=%async_computation.1 | async-start | bytes 1114112 | tf_op jit(solution)/shard_map/all_gather | solution.py:75
  8.8 168.8 %all-reduce.22.cloned.1.call-start = ((), (), s32[]{:S(2)}) async-start(), calls=%async_computation | async-start | bytes 2097152 | tf_op jit(solution)/shard_map/psum | solution.py:92
  12.2 114.0 %copy-start = (f32[256,512]{1,0:T(8,128)S(1)}, f32[256,512]{1,0:T(8,128)}, u32[]{:S(2)}) copy-start(f32[256,512]{1,0:T(8,128)} %param.10) | copy-start | bytes 1572868
  68.2 58.1 %copy-start.20 = (f32[1,2,256,512]{3,2,1,0:T(8,128)S(1)}, f32[1,2,256,512]{3,2,1,0:T(8,128)}, u32[]{:S(2)}) copy-start(f32[1,2,256,512]{3,2,1,0:T(8,128)} %all-gather.7.cloned.1.call-done) | copy-start | bytes 3145732
  69.3 61.0 %copy-start.7 = (f32[256,512]{1,0:T(8,128)}, f32[256,512]{1,0:T(8,128)S(1)}, u32[]{:S(2)}) copy-start(f32[256,512]{1,0:T(8,128)S(1)} %slice_bitcast_fusion.1) | copy-start | bytes 1572868
  126.2 4.1 %copy-start.9 = (f32[256,512]{1,0:T(8,128)}, f32[256,512]{1,0:T(8,128)S(1)}, u32[]{:S(2)}) copy-start(f32[256,512]{1,0:T(8,128)S(1)} %slice_bitcast_fusion.3) | copy-start | bytes 1572868
  128.2 2.8 %copy-start.2 = (f32[256,512]{1,0:T(8,128)}, f32[256,512]{1,0:T(8,128)S(1)}, u32[]{:S(2)}) copy-start(f32[256,512]{1,0:T(8,128)S(1)} %get-tuple-element.29) | copy-start | bytes 1572868
  129.1 4.2 %copy-start.13 = (f32[256,512]{1,0:T(8,128)}, f32[256,512]{1,0:T(8,128)S(1)}, u32[]{:S(2)}) copy-start(f32[256,512]{1,0:T(8,128)S(1)} %get-tuple-element.28) | copy-start | bytes 1572868
  130.3 4.3 %copy-start.15 = (f32[256,512]{1,0:T(8,128)}, f32[256,512]{1,0:T(8,128)S(1)}, u32[]{:S(2)}) copy-start(f32[256,512]{1,0:T(8,128)S(1)} %get-tuple-element.25) | copy-start | bytes 1572868
  130.3 4.3 %copy-start.17 = (f32[256,512]{1,0:T(8,128)}, f32[256,512]{1,0:T(8,128)S(1)}, u32[]{:S(2)}) copy-start(f32[256,512]{1,0:T(8,128)S(1)} %get-tuple-element.26) | copy-start | bytes 1572868
  134.3 3.6 %copy-start.5 = (f32[2,256,512]{2,1,0:T(8,128)}, f32[2,256,512]{2,1,0:T(8,128)S(1)}, u32[]{:S(2)}) copy-start(f32[2,256,512]{2,1,0:T(8,128)S(1)} %fusion.13) | copy-start | bytes 3145732
  149.4 4.7 %copy-start.3 = (f32[256,512]{1,0:T(8,128)S(1)}, f32[256,512]{1,0:T(8,128)}, u32[]{:S(2)}) copy-start(f32[256,512]{1,0:T(8,128)} %copy-done.2) | copy-start | bytes 1572868
  149.4 4.7 %copy-start.4 = (f32[2,256,512]{2,1,0:T(8,128)S(1)}, f32[2,256,512]{2,1,0:T(8,128)}, u32[]{:S(2)}) copy-start(f32[2,256,512]{2,1,0:T(8,128)} %get-tuple-element.24) | copy-start | bytes 3145732
  149.4 4.7 %copy-start.6 = (f32[2,256,512]{2,1,0:T(8,128)S(1)}, f32[2,256,512]{2,1,0:T(8,128)}, u32[]{:S(2)}) copy-start(f32[2,256,512]{2,1,0:T(8,128)} %get-tuple-element.8) | copy-start | bytes 3145732
  149.4 4.7 %copy-start.8 = (f32[256,512]{1,0:T(8,128)S(1)}, f32[256,512]{1,0:T(8,128)}, u32[]{:S(2)}) copy-start(f32[256,512]{1,0:T(8,128)} %copy-done.7) | copy-start | bytes 1572868
  149.4 4.7 %copy-start.10 = (f32[256,512]{1,0:T(8,128)S(1)}, f32[256,512]{1,0:T(8,128)}, u32[]{:S(2)}) copy-start(f32[256,512]{1,0:T(8,128)} %copy-done.9) | copy-start | bytes 1572868
  149.4 4.7 %copy-start.12 = (f32[256,512]{1,0:T(8,128)S(1)}, f32[256,512]{1,0:T(8,128)}, u32[]{:S(2)}) copy-start(f32[256,512]{1,0:T(8,128)} %copy-done.11) | copy-start | bytes 1572868
  149.4 4.7 %copy-start.14 = (f32[256,512]{1,0:T(8,128)S(1)}, f32[256,512]{1,0:T(8,128)}, u32[]{:S(2)}) copy-start(f32[256,512]{1,0:T(8,128)} %copy-done.13) | copy-start | bytes 1572868
  149.4 4.7 %copy-start.16 = (f32[256,512]{1,0:T(8,128)S(1)}, f32[256,512]{1,0:T(8,128)}, u32[]{:S(2)}) copy-start(f32[256,512]{1,0:T(8,128)} %copy-done.15) | copy-start | bytes 1572868
  149.4 4.7 %copy-start.18 = (f32[256,512]{1,0:T(8,128)S(1)}, f32[256,512]{1,0:T(8,128)}, u32[]{:S(2)}) copy-start(f32[256,512]{1,0:T(8,128)} %copy-done.17) | copy-start | bytes 1572868
  149.4 4.8 %copy-start.19 = (f32[2,256,512]{2,1,0:T(8,128)S(1)}, f32[2,256,512]{2,1,0:T(8,128)}, u32[]{:S(2)}) copy-start(f32[2,256,512]{2,1,0:T(8,128)} %get-tuple-element.5) | copy-start | bytes 3145732
  159.2 18.5 %copy-start.22 = (f32[2,128,512]{2,1,0:T(8,128)S(1)}, f32[2,128,512]{2,1,0:T(8,128)}, u32[]{:S(2)}) copy-start(f32[2,128,512]{2,1,0:T(8,128)} %param.9) | copy-start | bytes 1572868
  (3 other events, 6.2 us)
Sparse Core Ops, SparseCore 0:
  10.1 58.0 all-gather.6
  70.9 54.1 all-gather.4
  159.3 18.2 all-reduce.21
where the time goes:
time: 187 us; the launch traced here: 186 us
  waiting for transfers between devices  131 us (70%)
  other arithmetic  36.4 us (19%)
  between operations  13.5 us (7%)
  local copies, waits for them, and re-layouts  5.07 us (3%)
    all_gather x2, waiting for transfers between devices, on_device(): stored = lax.all_gather(checkpoints[member], 'probe', axis=1, tiled=True)  112 us
    mul x4, other arithmetic, hessian_term(): coefficient * upcoming  19.3 us
    psum x1, waiting for transfers between devices, on_device(): summed = lax.psum(accumulated, 'shot')  18.3 us
    add x1, other arithmetic, on_device(): accumulated + hessian_term(vectors, levels, coefficient, weight_square)  4.94 us
    add x3, other arithmetic, on_device(): 2.0 * current - before + coefficient * laplace(current)  3.89 us
  transfers between devices with their start and end apart: 3, of which 3 were waited for; matrix products, arithmetic and copies ran while one was open for 3% of the time, Pallas kernels for 0%

commit v1 on v0

--- a/solution.py
+++ b/solution.py
@@ -72,7 +72,28 @@
     weight_square = receiver * receiver
     accumulated = jnp.zeros_like(probes)
     for member in range(checkpoints.shape[0]):
-        stored = lax.all_gather(checkpoints[member], "probe", axis=1, tiled=True)
+        ways, here, step = (
+            lax.axis_size("probe"),
+            lax.axis_index("probe"),
+            checkpoints[member].shape[1],
+        )
+        lengths = [n * ways if d == 1 else n for d, n in enumerate(checkpoints[member].shape)]
+        stored = lax.dynamic_update_slice_in_dim(
+            jnp.zeros(lengths, checkpoints[member].dtype), checkpoints[member], here * step, axis=1
+        )
+        going_up = going_down = checkpoints[member]
+        for far in range(1, ways // 2 + 1):
+            going_up = lax.ppermute(going_up, "probe", [(d, (d + 1) % ways) for d in range(ways)])
+            stored = lax.dynamic_update_slice_in_dim(
+                stored, going_up, (here - far) % ways * step, axis=1
+            )
+            if 2 * far < ways:
+                going_down = lax.ppermute(
+                    going_down, "probe", [(d, (d - 1) % ways) for d in range(ways)]
+                )
+                stored = lax.dynamic_update_slice_in_dim(
+                    stored, going_down, (here + far) % ways * step, axis=1
+                )
         at_source = (jnp.arange(num_rows) == source_at).astype(jnp.float32)[:, None]
         before = stored[0]
         current = stored[1]

time: 187 us -> 173 us (0.925)
  waiting for transfers between devices: 131 us -> 23.8 us
  starting transfers between devices: 0.08 us -> 80.4 us
  local copies, waits for them, and re-layouts: 5.07 us -> 16.4 us
    all_gather x2 -> x0, waiting for transfers between devices: 112 us -> none  [on_device(): stored = lax.all_gather(checkpoints[member], 'probe', axis=1, tiled=True)]
    ppermute x0 -> x30, starting transfers between devices: none -> 80.4 us  [the longest x14 77 us: on_device(): lax.ppermute(going_down, 'probe', [(d, (d - 1) % ways) for d in range(way...]
    dynamic_update_slice x0 -> x32, local copies, waits for them, and re-layouts: none -> 10.4 us  [the longest x16 5.16 us: on_device(): lax.dynamic_update_slice_in_dim(stored, going_up, (here - far) % ways * s...]
    ppermute x0 -> x30, waiting for transfers between devices: none -> 7.46 us  [the longest x16 7.43 us: on_device(): lax.ppermute(going_up, 'probe', [(d, (d + 1) % ways) for d in range(ways)])]
    psum x1, waiting for transfers between devices: 18.3 us -> 16.3 us  [on_device(): summed = lax.psum(accumulated, 'shot')]
  transfers between devices with their start and end apart: 3 -> 31, of which waited for: 3 -> 3; matrix products, arithmetic and copies ran while one was open for 3% -> 9% of each run, Pallas kernels for 0% -> 0%
where the time goes in v1:
time: 173 us
  starting transfers between devices  80.4 us (46%)
  other arithmetic  37 us (21%)
  waiting for transfers between devices  23.8 us (14%)
  local copies, waits for them, and re-layouts  16.4 us (9%)
  between operations  14.2 us (8%)
    ppermute x14, starting transfers between devices, on_device(): lax.ppermute(going_down, 'probe', [(d, (d - 1) % ways) for d in range(way...  77 us
    mul x4, other arithmetic, hessian_term(): coefficient * upcoming  19.4 us
    psum x1, waiting for transfers between devices, on_device(): summed = lax.psum(accumulated, 'shot')  16.3 us
    ppermute x16, waiting for transfers between devices, on_device(): lax.ppermute(going_up, 'probe', [(d, (d + 1) % ways) for d in range(ways)])  7.43 us
    dynamic_update_slice x16, local copies, waits for them, and re-layouts, on_device(): lax.dynamic_update_slice_in_dim(stored, going_up, (here - far) % ways * s...  5.16 us
    add x1, other arithmetic, on_device(): accumulated + hessian_term(vectors, levels, coefficient, weight_square)  4.98 us
    add x3, other arithmetic, on_device(): 2.0 * current - before + coefficient * laplace(current)  4.79 us
    dynamic_update_slice x14, local copies, waits for them, and re-layouts, on_device(): lax.dynamic_update_slice_in_dim(stored, going_down, (here + far) % ways *...  4.57 us
  transfers between devices with their start and end apart: 31, of which 3 were waited for; matrix products, arithmetic and copies ran while one was open for 9% of the time, Pallas kernels for 0%

profile of v1, /device:TPU:0, one launch (start us, length us, event | category | flops | bytes accessed | tf_op | source)
XLA Modules:
  0.0 172.9 jit_solution(16138943688493683275)
XLA Ops:
  7.5 3.0 %collective-permute-start.15 = (f32[2,16,512]{2,1,0:T(8,128)S(1)}, f32[2,16,512]{2,1,0:T(8,128)S(1)}, u32[]{:S(2)}, u32[]{:S(2)}) collective-permute-start(f32[2,16,512]{2,1,0:T(8,128)S(1)} %get-tuple-element.32), channel_id=1, source_target_pairs={{0,1},{1,2},{2,3},{3,4},{4,5},{5,6},{6,7},{7,8},{8,9},{9,10},{10,1... | collective-permute-start | bytes 196616 | tf_op jit(solution)/shard_map/ppermute | solution.py:86
  10.5 4.1 %collective-permute-start.16 = (f32[2,16,512]{2,1,0:T(8,128)S(1)}, f32[2,16,512]{2,1,0:T(8,128)S(1)}, u32[]{:S(2)}, u32[]{:S(2)}) collective-permute-start(f32[2,16,512]{2,1,0:T(8,128)S(1)} %get-tuple-element.32), channel_id=1, source_target_pairs={{0,15},{1,0},{2,1},{3,2},{4,3},{5,4},{6,5},{7,6},{8,7},{9,8},{10,9... | collective-permute-start | bytes 196616 | tf_op jit(solution)/shard_map/ppermute | solution.py:91
  14.6 5.6 %collective-permute-start.1 = (f32[2,16,512]{2,1,0:T(8,128)S(1)}, f32[2,16,512]{2,1,0:T(8,128)S(1)}, u32[]{:S(2)}, u32[]{:S(2)}) collective-permute-start(f32[2,16,512]{2,1,0:T(8,128)S(1)} %get-tuple-element.33), channel_id=1, source_target_pairs={{0,15},{1,0},{2,1},{3,2},{4,3},{5,4},{6,5},{7,6},{8,7},{9,8},{10,9... | collective-permute-start | bytes 196616 | tf_op jit(solution)/shard_map/ppermute | solution.py:91
  25.0 5.6 %collective-permute-start.18 = (f32[2,16,512]{2,1,0:T(8,128)S(1)}, f32[2,16,512]{2,1,0:T(8,128)S(1)}, u32[]{:S(2)}, u32[]{:S(2)}) collective-permute-start(f32[2,16,512]{2,1,0:T(8,128)S(1)} %collective-permute-done.16), channel_id=1, source_target_pairs={{0,15},{1,0},{2,1},{3,2},{4,3},{5,4},{6,5},{7,6},{8,7},{9,8},{10,9... | collective-permute-start | bytes 196616 | tf_op jit(solution)/shard_map/ppermute | solution.py:91
  30.6 5.6 %collective-permute-start.3 = (f32[2,16,512]{2,1,0:T(8,128)S(1)}, f32[2,16,512]{2,1,0:T(8,128)S(1)}, u32[]{:S(2)}, u32[]{:S(2)}) collective-permute-start(f32[2,16,512]{2,1,0:T(8,128)S(1)} %collective-permute-done.1), channel_id=1, source_target_pairs={{0,15},{1,0},{2,1},{3,2},{4,3},{5,4},{6,5},{7,6},{8,7},{9,8},{10,9... | collective-permute-start | bytes 196616 | tf_op jit(solution)/shard_map/ppermute | solution.py:91
  37.6 5.6 %collective-permute-start.20 = (f32[2,16,512]{2,1,0:T(8,128)S(1)}, f32[2,16,512]{2,1,0:T(8,128)S(1)}, u32[]{:S(2)}, u32[]{:S(2)}) collective-permute-start(f32[2,16,512]{2,1,0:T(8,128)S(1)} %collective-permute-done.18), channel_id=1, source_target_pairs={{0,15},{1,0},{2,1},{3,2},{4,3},{5,4},{6,5},{7,6},{8,7},{9,8},{10,9... | collective-permute-start | bytes 196616 | tf_op jit(solution)/shard_map/ppermute | solution.py:91
  43.2 5.6 %collective-permute-start.5 = (f32[2,16,512]{2,1,0:T(8,128)S(1)}, f32[2,16,512]{2,1,0:T(8,128)S(1)}, u32[]{:S(2)}, u32[]{:S(2)}) collective-permute-start(f32[2,16,512]{2,1,0:T(8,128)S(1)} %collective-permute-done.3), channel_id=1, source_target_pairs={{0,15},{1,0},{2,1},{3,2},{4,3},{5,4},{6,5},{7,6},{8,7},{9,8},{10,9... | collective-permute-start | bytes 196616 | tf_op jit(solution)/shard_map/ppermute | solution.py:91
  50.2 5.6 %collective-permute-start.22 = (f32[2,16,512]{2,1,0:T(8,128)S(1)}, f32[2,16,512]{2,1,0:T(8,128)S(1)}, u32[]{:S(2)}, u32[]{:S(2)}) collective-permute-start(f32[2,16,512]{2,1,0:T(8,128)S(1)} %collective-permute-done.20), channel_id=1, source_target_pairs={{0,15},{1,0},{2,1},{3,2},{4,3},{5,4},{6,5},{7,6},{8,7},{9,8},{10,9... | collective-permute-start | bytes 196616 | tf_op jit(solution)/shard_map/ppermute | solution.py:91
  55.8 5.6 %collective-permute-start.7 = (f32[2,16,512]{2,1,0:T(8,128)S(1)}, f32[2,16,512]{2,1,0:T(8,128)S(1)}, u32[]{:S(2)}, u32[]{:S(2)}) collective-permute-start(f32[2,16,512]{2,1,0:T(8,128)S(1)} %collective-permute-done.5), channel_id=1, source_target_pairs={{0,15},{1,0},{2,1},{3,2},{4,3},{5,4},{6,5},{7,6},{8,7},{9,8},{10,9... | collective-permute-start | bytes 196616 | tf_op jit(solution)/shard_map/ppermute | solution.py:91
  62.8 5.6 %collective-permute-start.24 = (f32[2,16,512]{2,1,0:T(8,128)S(1)}, f32[2,16,512]{2,1,0:T(8,128)S(1)}, u32[]{:S(2)}, u32[]{:S(2)}) collective-permute-start(f32[2,16,512]{2,1,0:T(8,128)S(1)} %collective-permute-done.22), channel_id=1, source_target_pairs={{0,15},{1,0},{2,1},{3,2},{4,3},{5,4},{6,5},{7,6},{8,7},{9,8},{10,9... | collective-permute-start | bytes 196616 | tf_op jit(solution)/shard_map/ppermute | solution.py:91
  68.5 5.6 %collective-permute-start.9 = (f32[2,16,512]{2,1,0:T(8,128)S(1)}, f32[2,16,512]{2,1,0:T(8,128)S(1)}, u32[]{:S(2)}, u32[]{:S(2)}) collective-permute-start(f32[2,16,512]{2,1,0:T(8,128)S(1)} %collective-permute-done.7), channel_id=1, source_target_pairs={{0,15},{1,0},{2,1},{3,2},{4,3},{5,4},{6,5},{7,6},{8,7},{9,8},{10,9... | collective-permute-start | bytes 196616 | tf_op jit(solution)/shard_map/ppermute | solution.py:91
  75.5 5.6 %collective-permute-start.26 = (f32[2,16,512]{2,1,0:T(8,128)S(1)}, f32[2,16,512]{2,1,0:T(8,128)S(1)}, u32[]{:S(2)}, u32[]{:S(2)}) collective-permute-start(f32[2,16,512]{2,1,0:T(8,128)S(1)} %collective-permute-done.24), channel_id=1, source_target_pairs={{0,15},{1,0},{2,1},{3,2},{4,3},{5,4},{6,5},{7,6},{8,7},{9,8},{10,9... | collective-permute-start | bytes 196616 | tf_op jit(solution)/shard_map/ppermute | solution.py:91
  81.1 5.6 %collective-permute-start.11 = (f32[2,16,512]{2,1,0:T(8,128)S(1)}, f32[2,16,512]{2,1,0:T(8,128)S(1)}, u32[]{:S(2)}, u32[]{:S(2)}) collective-permute-start(f32[2,16,512]{2,1,0:T(8,128)S(1)} %collective-permute-done.9), channel_id=1, source_target_pairs={{0,15},{1,0},{2,1},{3,2},{4,3},{5,4},{6,5},{7,6},{8,7},{9,8},{10,9... | collective-permute-start | bytes 196616 | tf_op jit(solution)/shard_map/ppermute | solution.py:91
  88.1 5.6 %collective-permute-start.28 = (f32[2,16,512]{2,1,0:T(8,128)S(1)}, f32[2,16,512]{2,1,0:T(8,128)S(1)}, u32[]{:S(2)}, u32[]{:S(2)}) collective-permute-start(f32[2,16,512]{2,1,0:T(8,128)S(1)} %collective-permute-done.26), channel_id=1, source_target_pairs={{0,15},{1,0},{2,1},{3,2},{4,3},{5,4},{6,5},{7,6},{8,7},{9,8},{10,9... | collective-permute-start | bytes 196616 | tf_op jit(solution)/shard_map/ppermute | solution.py:91
  93.7 5.6 %collective-permute-start.13 = (f32[2,16,512]{2,1,0:T(8,128)S(1)}, f32[2,16,512]{2,1,0:T(8,128)S(1)}, u32[]{:S(2)}, u32[]{:S(2)}) collective-permute-start(f32[2,16,512]{2,1,0:T(8,128)S(1)} %collective-permute-done.11), channel_id=1, source_target_pairs={{0,15},{1,0},{2,1},{3,2},{4,3},{5,4},{6,5},{7,6},{8,7},{9,8},{10,9... | collective-permute-start | bytes 196616 | tf_op jit(solution)/shard_map/ppermute | solution.py:91
  102.9 6.5 %collective-permute-done.14 = f32[2,16,512]{2,1,0:T(8,128)S(1)} collective-permute-done((f32[2,16,512]{2,1,0:T(8,128)S(1)}, f32[2,16,512]{2,1,0:T(8,128)S(1)}, u32[]{:S(2)}, u32[]{:S(2)}) %collective-permute-start.14) | collective-permute-done | bytes 65568 | tf_op jit(solution)/shard_map/ppermute | solution.py:86
  111.3 2.1 %fusion.120 = (f32[256,512]{1,0:T(8,128)S(1)}, f32[256,512]{1,0:T(8,128)S(1)}) fusion(f32[256,512]{1,0:T(8,128)S(1)} %copy-done, f32[256,512]{1,0:T(8,128)S(1)} %slice_bitcast_fusion.1, f32[2,256,512]{2,1,0:T(8,128)S(1)} %constant_dynamic-update-slice_fusion, f32[512]{0:T(512)S(1)} %bitcast.39, f32[256]{0:T(256)S(1)} %compare_convert_fusion.1, ...), kind=kLoop, calls=%fused_computation.202 | loop fusion | flops 2883584 | bytes 3675136 | tf_op jit(solution)/shard_map/add | solution.py:103
  122.9 3.3 %broadcast_multiply_fusion.2 = (f32[2,256,512]{2,1,0:T(8,128)S(1)}, f32[2,256,512]{2,1,0:T(8,128)S(1)}, f32[2,256,512]{2,1,0:T(8,128)}, f32[2,256,512]{2,1,0:T(8,128)S(1)}) fusion(f32[256,512]{1,0:T(8,128)S(1)} %copy-done, f32[256,512]{1,0:T(8,128)S(1)} %fusion.113, f32[256,512]{1,0:T(8,128)S(1)} %get-tuple-element.25, f32[2,256,512]{2,1,0:T(8,128)S(1)} %copy-done.1, ...), kind=kLoop, calls=%fused_computation.226 | loop fusion | flops 7602176 | bytes 12060672 | tf_op jit(solution)/shard_map/mul | solution.py:54
  126.2 2.1 %broadcast_multiply_fusion.1 = (f32[2,256,512]{2,1,0:T(8,128)}, f32[2,256,512]{2,1,0:T(8,128)}) fusion(f32[256,512]{1,0:T(8,128)S(1)} %copy-done, f32[2,256,512]{2,1,0:T(8,128)S(1)} %get-tuple-element.9, f32[2,256,512]{2,1,0:T(8,128)S(1)} %get-tuple-element.10, f32[2,256,512]{2,1,0:T(8,128)S(1)} %get-tuple-element.21, f32[256,512]{1,0:T(8,128)S(1)} %mul.631), kind=kLoop, calls=%fused_computation.225 | loop fusion | flops 2621440 | bytes 6291456 | tf_op jit(solution)/shard_map/mul | solution.py:54
  128.3 9.4 %broadcast_multiply_fusion = (f32[2,256,512]{2,1,0:T(8,128)}, f32[2,256,512]{2,1,0:T(8,128)}, f32[2,256,512]{2,1,0:T(8,128)}, f32[2,256,512]{2,1,0:T(8,128)}) fusion(f32[256,512]{1,0:T(8,128)S(1)} %copy-done, f32[2,256,512]{2,1,0:T(8,128)S(1)} %get-tuple-element.10, f32[2,256,512]{2,1,0:T(8,128)} %get-tuple-element.7, f32[2,256,512]{2,1,0:T(8,128)} %get-tuple-element.8, ...), kind=kLoop, calls=%fused_computation.224 | loop fusion | flops 5505024 | bytes 12582912 | tf_op jit(solution)/shard_map/mul | solution.py:54
  137.8 4.7 %broadcast_multiply_fusion.3 = (f32[2,256,512]{2,1,0:T(8,128)S(1)}, f32[2,256,512]{2,1,0:T(8,128)S(1)}) fusion(f32[256,512]{1,0:T(8,128)S(1)} %copy-done, f32[2,256,512]{2,1,0:T(8,128)S(1)} %get-tuple-element.18, f32[2,256,512]{2,1,0:T(8,128)} %get-tuple-element.23, f32[2,256,512]{2,1,0:T(8,128)} %get-tuple-element.24, ...), kind=kLoop, calls=%fused_computation.227 | loop fusion | flops 2883584 | bytes 7340032 | tf_op jit(solution)/shard_map/mul | solution.py:54
  142.6 5.0 %fusion.42 = f32[2,256,512]{2,1,0:T(8,128)} fusion(f32[2,256,512]{2,1,0:T(8,128)S(1)} %copy-done.4, f32[2,256,512]{2,1,0:T(8,128)S(1)} %get-tuple-element.11, f32[2,256,512]{2,1,0:T(8,128)S(1)} %copy-done.6, f32[2,256,512]{2,1,0:T(8,128)S(1)} %copy-done.21, f32[2,256,512]{2,1,0:T(8,128)} %get-tuple-element.6, f32[2,256,512]{2,1,0:T(8,128)S(1)} %get-tuple-element.19, ...), kind=kLoop, calls=%fused_computation.94 | loop fusion | flops 9175040 | bytes 16252928 | tf_op jit(solution)/shard_map/add | solution.py:111
  147.8 16.3 %all-reduce.22.cloned.1.call-done = f32[2,256,512]{2,1,0:T(8,128)} async-done(((f32[2,256,512]{2,1,0:T(8,128)}), f32[2,256,512]{2,1,0:T(8,128)}) %all-reduce.22.cloned.1.call-update) | async-done | bytes 1048592 | tf_op jit(solution)/shard_map/psum | solution.py:113
  164.1 1.9 %subtract_multiply_fusion = f32[2,128,512]{2,1,0:T(8,128)} fusion(f32[2,128,512]{2,1,0:T(8,128)S(1)} %copy-done.23, f32[2,256,512]{2,1,0:T(8,128)} %all-reduce.22.cloned.1.call-done, s32[]{:T(128)S(6)} %select_n.236, f32[2,128]{1,0:T(2,128)S(1)} %compare_convert_fusion.2), kind=kLoop, calls=%fused_computation.223 | loop fusion | flops 262144 | bytes 1573892 | tf_op jit(solution)/shard_map/mul | solution.py:117
  (156 shorter events, 27.3 us)
Async XLA Ops:
  6.5 157.5 %all-reduce.22.cloned.1.call-start = ((), (), s32[]{:S(2)}) async-start(), calls=%async_computation | async-start | bytes 2097152 | tf_op jit(solution)/shard_map/psum | solution.py:113
  7.5 17.4 %collective-permute-start.15 = (f32[2,16,512]{2,1,0:T(8,128)S(1)}, f32[2,16,512]{2,1,0:T(8,128)S(1)}, u32[]{:S(2)}, u32[]{:S(2)}) collective-permute-start(f32[2,16,512]{2,1,0:T(8,128)S(1)} %get-tuple-element.32), channel_id=1, source_target_pairs={{0,1},{1,2},{2,3},{3,4},{4,5},{5,6},{6,7},{7,8},{8,9},{9,10},{10,1... | collective-permute-start | bytes 196616 | tf_op jit(solution)/shard_map/ppermute | solution.py:86
  10.5 14.5 %collective-permute-start.16 = (f32[2,16,512]{2,1,0:T(8,128)S(1)}, f32[2,16,512]{2,1,0:T(8,128)S(1)}, u32[]{:S(2)}, u32[]{:S(2)}) collective-permute-start(f32[2,16,512]{2,1,0:T(8,128)S(1)} %get-tuple-element.32), channel_id=1, source_target_pairs={{0,15},{1,0},{2,1},{3,2},{4,3},{5,4},{6,5},{7,6},{8,7},{9,8},{10,9... | collective-permute-start | bytes 196616 | tf_op jit(solution)/shard_map/ppermute | solution.py:91
  14.6 16.0 %collective-permute-start = (f32[2,16,512]{2,1,0:T(8,128)S(1)}, f32[2,16,512]{2,1,0:T(8,128)S(1)}, u32[]{:S(2)}, u32[]{:S(2)}) collective-permute-start(f32[2,16,512]{2,1,0:T(8,128)S(1)} %get-tuple-element.33), channel_id=1, source_target_pairs={{0,1},{1,2},{2,3},{3,4},{4,5},{5,6},{6,7},{7,8},{8,9},{9,10},{10,1... | collective-permute-start | bytes 196616 | tf_op jit(solution)/shard_map/ppermute | solution.py:86
  14.6 16.0 %collective-permute-start.1 = (f32[2,16,512]{2,1,0:T(8,128)S(1)}, f32[2,16,512]{2,1,0:T(8,128)S(1)}, u32[]{:S(2)}, u32[]{:S(2)}) collective-permute-start(f32[2,16,512]{2,1,0:T(8,128)S(1)} %get-tuple-element.33), channel_id=1, source_target_pairs={{0,15},{1,0},{2,1},{3,2},{4,3},{5,4},{6,5},{7,6},{8,7},{9,8},{10,9... | collective-permute-start | bytes 196616 | tf_op jit(solution)/shard_map/ppermute | solution.py:91
  25.0 12.6 %collective-permute-start.18 = (f32[2,16,512]{2,1,0:T(8,128)S(1)}, f32[2,16,512]{2,1,0:T(8,128)S(1)}, u32[]{:S(2)}, u32[]{:S(2)}) collective-permute-start(f32[2,16,512]{2,1,0:T(8,128)S(1)} %collective-permute-done.16), channel_id=1, source_target_pairs={{0,15},{1,0},{2,1},{3,2},{4,3},{5,4},{6,5},{7,6},{8,7},{9,8},{10,9... | collective-permute-start | bytes 196616 | tf_op jit(solution)/shard_map/ppermute | solution.py:91
  30.6 12.6 %collective-permute-start.2 = (f32[2,16,512]{2,1,0:T(8,128)S(1)}, f32[2,16,512]{2,1,0:T(8,128)S(1)}, u32[]{:S(2)}, u32[]{:S(2)}) collective-permute-start(f32[2,16,512]{2,1,0:T(8,128)S(1)} %collective-permute-done), channel_id=1, source_target_pairs={{0,1},{1,2},{2,3},{3,4},{4,5},{5,6},{6,7},{7,8},{8,9},{9,10},{10,1... | collective-permute-start | bytes 196616 | tf_op jit(solution)/shard_map/ppermute | solution.py:86
  30.6 12.6 %collective-permute-start.3 = (f32[2,16,512]{2,1,0:T(8,128)S(1)}, f32[2,16,512]{2,1,0:T(8,128)S(1)}, u32[]{:S(2)}, u32[]{:S(2)}) collective-permute-start(f32[2,16,512]{2,1,0:T(8,128)S(1)} %collective-permute-done.1), channel_id=1, source_target_pairs={{0,15},{1,0},{2,1},{3,2},{4,3},{5,4},{6,5},{7,6},{8,7},{9,8},{10,9... | collective-permute-start | bytes 196616 | tf_op jit(solution)/shard_map/ppermute | solution.py:91
  37.5 12.6 %collective-permute-start.19 = (f32[2,16,512]{2,1,0:T(8,128)S(1)}, f32[2,16,512]{2,1,0:T(8,128)S(1)}, u32[]{:S(2)}, u32[]{:S(2)}) collective-permute-start(f32[2,16,512]{2,1,0:T(8,128)S(1)} %collective-permute-done.17), channel_id=1, source_target_pairs={{0,1},{1,2},{2,3},{3,4},{4,5},{5,6},{6,7},{7,8},{8,9},{9,10},{10,1... | collective-permute-start | bytes 196616 | tf_op jit(solution)/shard_map/ppermute | solution.py:86
  37.6 12.6 %collective-permute-start.20 = (f32[2,16,512]{2,1,0:T(8,128)S(1)}, f32[2,16,512]{2,1,0:T(8,128)S(1)}, u32[]{:S(2)}, u32[]{:S(2)}) collective-permute-start(f32[2,16,512]{2,1,0:T(8,128)S(1)} %collective-permute-done.18), channel_id=1, source_target_pairs={{0,15},{1,0},{2,1},{3,2},{4,3},{5,4},{6,5},{7,6},{8,7},{9,8},{10,9... | collective-permute-start | bytes 196616 | tf_op jit(solution)/shard_map/ppermute | solution.py:91
  43.2 12.6 %collective-permute-start.4 = (f32[2,16,512]{2,1,0:T(8,128)S(1)}, f32[2,16,512]{2,1,0:T(8,128)S(1)}, u32[]{:S(2)}, u32[]{:S(2)}) collective-permute-start(f32[2,16,512]{2,1,0:T(8,128)S(1)} %collective-permute-done.2), channel_id=1, source_target_pairs={{0,1},{1,2},{2,3},{3,4},{4,5},{5,6},{6,7},{7,8},{8,9},{9,10},{10,1... | collective-permute-start | bytes 196616 | tf_op jit(solution)/shard_map/ppermute | solution.py:86
  43.2 12.6 %collective-permute-start.5 = (f32[2,16,512]{2,1,0:T(8,128)S(1)}, f32[2,16,512]{2,1,0:T(8,128)S(1)}, u32[]{:S(2)}, u32[]{:S(2)}) collective-permute-start(f32[2,16,512]{2,1,0:T(8,128)S(1)} %collective-permute-done.3), channel_id=1, source_target_pairs={{0,15},{1,0},{2,1},{3,2},{4,3},{5,4},{6,5},{7,6},{8,7},{9,8},{10,9... | collective-permute-start | bytes 196616 | tf_op jit(solution)/shard_map/ppermute | solution.py:91
  50.1 12.6 %collective-permute-start.21 = (f32[2,16,512]{2,1,0:T(8,128)S(1)}, f32[2,16,512]{2,1,0:T(8,128)S(1)}, u32[]{:S(2)}, u32[]{:S(2)}) collective-permute-start(f32[2,16,512]{2,1,0:T(8,128)S(1)} %collective-permute-done.19), channel_id=1, source_target_pairs={{0,1},{1,2},{2,3},{3,4},{4,5},{5,6},{6,7},{7,8},{8,9},{9,10},{10,1... | collective-permute-start | bytes 196616 | tf_op jit(solution)/shard_map/ppermute | solution.py:86
  50.2 12.6 %collective-permute-start.22 = (f32[2,16,512]{2,1,0:T(8,128)S(1)}, f32[2,16,512]{2,1,0:T(8,128)S(1)}, u32[]{:S(2)}, u32[]{:S(2)}) collective-permute-start(f32[2,16,512]{2,1,0:T(8,128)S(1)} %collective-permute-done.20), channel_id=1, source_target_pairs={{0,15},{1,0},{2,1},{3,2},{4,3},{5,4},{6,5},{7,6},{8,7},{9,8},{10,9... | collective-permute-start | bytes 196616 | tf_op jit(solution)/shard_map/ppermute | solution.py:91
  55.8 12.6 %collective-permute-start.6 = (f32[2,16,512]{2,1,0:T(8,128)S(1)}, f32[2,16,512]{2,1,0:T(8,128)S(1)}, u32[]{:S(2)}, u32[]{:S(2)}) collective-permute-start(f32[2,16,512]{2,1,0:T(8,128)S(1)} %collective-permute-done.4), channel_id=1, source_target_pairs={{0,1},{1,2},{2,3},{3,4},{4,5},{5,6},{6,7},{7,8},{8,9},{9,10},{10,1... | collective-permute-start | bytes 196616 | tf_op jit(solution)/shard_map/ppermute | solution.py:86
  55.8 12.6 %collective-permute-start.7 = (f32[2,16,512]{2,1,0:T(8,128)S(1)}, f32[2,16,512]{2,1,0:T(8,128)S(1)}, u32[]{:S(2)}, u32[]{:S(2)}) collective-permute-start(f32[2,16,512]{2,1,0:T(8,128)S(1)} %collective-permute-done.5), channel_id=1, source_target_pairs={{0,15},{1,0},{2,1},{3,2},{4,3},{5,4},{6,5},{7,6},{8,7},{9,8},{10,9... | collective-permute-start | bytes 196616 | tf_op jit(solution)/shard_map/ppermute | solution.py:91
  62.8 12.6 %collective-permute-start.23 = (f32[2,16,512]{2,1,0:T(8,128)S(1)}, f32[2,16,512]{2,1,0:T(8,128)S(1)}, u32[]{:S(2)}, u32[]{:S(2)}) collective-permute-start(f32[2,16,512]{2,1,0:T(8,128)S(1)} %collective-permute-done.21), channel_id=1, source_target_pairs={{0,1},{1,2},{2,3},{3,4},{4,5},{5,6},{6,7},{7,8},{8,9},{9,10},{10,1... | collective-permute-start | bytes 196616 | tf_op jit(solution)/shard_map/ppermute | solution.py:86
  62.8 12.6 %collective-permute-start.24 = (f32[2,16,512]{2,1,0:T(8,128)S(1)}, f32[2,16,512]{2,1,0:T(8,128)S(1)}, u32[]{:S(2)}, u32[]{:S(2)}) collective-permute-start(f32[2,16,512]{2,1,0:T(8,128)S(1)} %collective-permute-done.22), channel_id=1, source_target_pairs={{0,15},{1,0},{2,1},{3,2},{4,3},{5,4},{6,5},{7,6},{8,7},{9,8},{10,9... | collective-permute-start | bytes 196616 | tf_op jit(solution)/shard_map/ppermute | solution.py:91
  68.5 12.6 %collective-permute-start.8 = (f32[2,16,512]{2,1,0:T(8,128)S(1)}, f32[2,16,512]{2,1,0:T(8,128)S(1)}, u32[]{:S(2)}, u32[]{:S(2)}) collective-permute-start(f32[2,16,512]{2,1,0:T(8,128)S(1)} %collective-permute-done.6), channel_id=1, source_target_pairs={{0,1},{1,2},{2,3},{3,4},{4,5},{5,6},{6,7},{7,8},{8,9},{9,10},{10,1... | collective-permute-start | bytes 196616 | tf_op jit(solution)/shard_map/ppermute | solution.py:86
  68.5 12.6 %collective-permute-start.9 = (f32[2,16,512]{2,1,0:T(8,128)S(1)}, f32[2,16,512]{2,1,0:T(8,128)S(1)}, u32[]{:S(2)}, u32[]{:S(2)}) collective-permute-start(f32[2,16,512]{2,1,0:T(8,128)S(1)} %collective-permute-done.7), channel_id=1, source_target_pairs={{0,15},{1,0},{2,1},{3,2},{4,3},{5,4},{6,5},{7,6},{8,7},{9,8},{10,9... | collective-permute-start | bytes 196616 | tf_op jit(solution)/shard_map/ppermute | solution.py:91
  81.1 12.6 %collective-permute-start.10 = (f32[2,16,512]{2,1,0:T(8,128)S(1)}, f32[2,16,512]{2,1,0:T(8,128)S(1)}, u32[]{:S(2)}, u32[]{:S(2)}) collective-permute-start(f32[2,16,512]{2,1,0:T(8,128)S(1)} %collective-permute-done.8), channel_id=1, source_target_pairs={{0,1},{1,2},{2,3},{3,4},{4,5},{5,6},{6,7},{7,8},{8,9},{9,10},{10,1... | collective-permute-start | bytes 196616 | tf_op jit(solution)/shard_map/ppermute | solution.py:86
  81.1 12.6 %collective-permute-start.11 = (f32[2,16,512]{2,1,0:T(8,128)S(1)}, f32[2,16,512]{2,1,0:T(8,128)S(1)}, u32[]{:S(2)}, u32[]{:S(2)}) collective-permute-start(f32[2,16,512]{2,1,0:T(8,128)S(1)} %collective-permute-done.9), channel_id=1, source_target_pairs={{0,15},{1,0},{2,1},{3,2},{4,3},{5,4},{6,5},{7,6},{8,7},{9,8},{10,9... | collective-permute-start | bytes 196616 | tf_op jit(solution)/shard_map/ppermute | solution.py:91
  88.0 12.6 %collective-permute-start.27 = (f32[2,16,512]{2,1,0:T(8,128)S(1)}, f32[2,16,512]{2,1,0:T(8,128)S(1)}, u32[]{:S(2)}, u32[]{:S(2)}) collective-permute-start(f32[2,16,512]{2,1,0:T(8,128)S(1)} %collective-permute-done.25), channel_id=1, source_target_pairs={{0,1},{1,2},{2,3},{3,4},{4,5},{5,6},{6,7},{7,8},{8,9},{9,10},{10,1... | collective-permute-start | bytes 196616 | tf_op jit(solution)/shard_map/ppermute | solution.py:86
  88.1 14.8 %collective-permute-start.28 = (f32[2,16,512]{2,1,0:T(8,128)S(1)}, f32[2,16,512]{2,1,0:T(8,128)S(1)}, u32[]{:S(2)}, u32[]{:S(2)}) collective-permute-start(f32[2,16,512]{2,1,0:T(8,128)S(1)} %collective-permute-done.26), channel_id=1, source_target_pairs={{0,15},{1,0},{2,1},{3,2},{4,3},{5,4},{6,5},{7,6},{8,7},{9,8},{10,9... | collective-permute-start | bytes 196616 | tf_op jit(solution)/shard_map/ppermute | solution.py:91
  (32 other events, 183.9 us)
Sparse Core Ops, SparseCore 0:
  147.7 16.3 all-reduce.21
